TPU v7x, 128 devices: a whole 4x4x4 slice. The times are simulated.
128 devices in a mesh: cell: 16 (over x, z_hi, core), tm: 8 (over y, z_lo).
Axes of the slice: x: 4, y: 4, z: 4 (z_hi: 2, z_lo: 2; z = z_hi * 2 + z_lo), core: 2. Of those that a mesh axis runs over, the one named last changes fastest.
Arguments:
- window: float32 [16384, 16384], P('cell', 'tm'), may hold values from -0.09375 to 0.09375
- range_test: float32 [16384, 256], P('tm'), may hold values from -0.046875 to 0.046875
- co_test: float32 [256, 16384], P(None, 'cell'), may hold values from -0.046875 to 0.046875
- core_left: float32 [512, 16384], P(None, 'cell'), may hold values from -0.046875 to 0.046875
- core_right: float32 [512, 16384], P(None, 'tm'), may hold values from -0.046875 to 0.046875
Outputs:
- range_basis: float32 [16384, 256], P('cell')
- co_basis: float32 [256, 16384], P(None, 'tm')
- core: float32 [256, 256], replicated
All inputs are finite; a program needn't handle non-finite values.
Results may differ from a plain program's by a relative error of at most 0.00023.
Values sent between devices are 32-bit elements; how exact they have to be, the bound alone decides.
A program may use at most 128 MiB of HBM per device.

v0:
```python
import math
import jax
import jax.numpy as jnp
from jax import lax
from jax.sharding import PartitionSpec as P


def inner_rows(left, right):
    return lax.dot_general(left, right, (((0,), (0,)), ((), ())), precision=lax.Precision.HIGHEST)


def inner_cols(left, right):
    return lax.dot_general(left, right, (((1,), (1,)), ((), ())), precision=lax.Precision.HIGHEST)


def product(left, right):
    return jnp.dot(left, right, precision=lax.Precision.HIGHEST, preferred_element_type=jnp.float32)


def per_device(window, range_test, co_test, core_left, core_right):
    rows_total = window.shape[0] * lax.axis_size("cell")
    cols_total = window.shape[1] * lax.axis_size("tm")
    range_term = product(window, range_test)
    co_term = product(co_test, window)
    left_window = product(core_left, window)
    core_term = inner_cols(left_window, core_right)
    sketch_z = lax.psum(core_term, ("cell", "tm"))
    range_full = lax.psum(range_term, "tm")
    co_full = lax.psum(co_term, "cell")
    gram_y = lax.psum(inner_rows(range_full, range_full) / rows_total, "cell")
    gram_w = lax.psum(inner_cols(co_full, co_full) / cols_total, "tm")
    lower_y = jnp.linalg.cholesky(gram_y)
    lower_w = jnp.linalg.cholesky(gram_w)
    range_basis = jax.scipy.linalg.solve_triangular(lower_y, range_full.T, lower=True).T
    co_basis = jax.scipy.linalg.solve_triangular(lower_w, co_full, lower=True)
    left_image = lax.psum(product(core_left, range_basis), "cell")
    right_image = lax.psum(inner_cols(core_right, co_basis), "tm")
    gram_left = inner_rows(left_image, left_image)
    gram_right = inner_rows(right_image, right_image)
    projected = inner_rows(left_image, sketch_z)
    left_solved = jax.scipy.linalg.cho_solve((jnp.linalg.cholesky(gram_left), True), projected)
    middle = product(left_solved, right_image)
    core = jax.scipy.linalg.cho_solve((jnp.linalg.cholesky(gram_right), True), middle.T).T
    core = core * math.sqrt(rows_total * cols_total)
    return (range_basis, co_basis, core)


def solution(mesh):
    return jax.shard_map(
        per_device,
        mesh=mesh,
        in_specs=(P("cell", "tm"), P("tm", None), P(None, "cell"), P(None, "cell"), P(None, "tm")),
        out_specs=(P("cell", None), P(None, "tm"), P()),
        check_vma=False,
    )
```

profile of v0, /device:TPU:0, one launch (start us, length us, event | category | flops | bytes accessed | tf_op | source)
XLA Modules:
  0.0 920.8 jit_solution(13198876106782574047)
XLA Ops:
  7.2 10.7 %fusion.50 = f32[1024,256]{1,0:T(8,128)} fusion(f32[1024,2048]{1,0:T(8,128)} %param.6, f32[2048,256]{1,0:T(8,128)} %param.7), kind=kOutput, calls=%fused_computation.123 | convolution fusion | flops 6442450944 | bytes 11534336 | tf_op jit(solution)/shard_map/dot_general | solution.py:17
  18.0 80.7 %all-reduce.9.cloned.1.call-done = f32[1024,256]{1,0:T(8,128)} async-done(((f32[1024,256]{1,0:T(8,128)}), f32[1024,256]{1,0:T(8,128)}) %all-reduce.9.cloned.1.call-update) | async-done | bytes 1048592 | tf_op jit(solution)/shard_map/psum | solution.py:28
  98.6 4.1 convolution_multiply_fusion.1
  102.8 10.7 %fusion.51 = f32[256,2048]{1,0:T(8,128)} fusion(f32[256,1024]{1,0:T(8,128)S(1)} %copy-done.12, f32[1024,2048]{1,0:T(8,128)} %param.6), kind=kOutput, calls=%fused_computation.124 | convolution fusion | flops 6442450944 | bytes 11534336 | tf_op jit(solution)/shard_map/dot_general | solution.py:17
  113.5 127.4 %all-reduce.11.cloned.1.call-done = f32[256,256]{0,1:T(8,128)} async-done(((f32[256,256]{0,1:T(8,128)}), f32[256,256]{0,1:T(8,128)}) %all-reduce.11.cloned.1.call-update) | async-done | bytes 262160 | tf_op jit(solution)/shard_map/psum | solution.py:30
  243.7 11.7 %cholesky.214 = f32[128,128]{1,0:T(8,128)S(1)} custom-call(f32[128,128]{1,0:T(8,128)S(1)} %cholesky.346), custom_call_target="Cholesky" | custom-call | tf_op jit(solution)/shard_map/jit(cholesky)/cholesky | solution.py:32
  255.5 9.8 %custom-call.37 = f32[1,128,128]{1,2,0:T(8,128)S(1)} custom-call(f32[1,128,128]{2,1,0:T(8,128)S(1)} %get-tuple-element.96), custom_call_target="InvertDiagBlocksLowerTriangular" | custom-call | tf_op jit(solution)/shard_map/jit(cholesky)/cholesky | solution.py:32
  267.4 11.7 %cholesky.231 = f32[128,128]{1,0:T(8,128)S(1)} custom-call(f32[128,128]{1,0:T(8,128)S(1)} %convolution_subtract_fusion.9), custom_call_target="Cholesky" | custom-call | tf_op jit(solution)/shard_map/jit(cholesky)/cholesky | solution.py:32
  282.3 4.1 while.4
  282.9 1.4 bitcast_dynamic-update-slice_fusion.8
  284.9 1.4 bitcast_dynamic-update-slice_fusion.8
  287.0 20.7 %custom-call.30 = f32[2,128,128]{1,2,0:T(8,128)S(1)} custom-call(f32[2,128,128]{2,1,0:T(8,128)} %copy-done.17), custom_call_target="InvertDiagBlocksLowerTriangular" | custom-call | tf_op jit(solution)/shard_map/jit(_solve_triangular)/triangular_solve | solution.py:34
  310.0 2.8 convolution_bitcast_fusion
  312.9 16.9 %fusion.54 = f32[512,2048]{1,0:T(8,128)S(1)} fusion(f32[512,1024]{1,0:T(8,128)S(1)} %copy-done, f32[1024,2048]{1,0:T(8,128)} %param.6), kind=kOutput, calls=%fused_computation.127 | convolution fusion | flops 12884901888 | bytes 14680064 | tf_op jit(solution)/shard_map/dot_general | solution.py:17
  329.8 7.9 fusion.55
  337.7 2.8 all-reduce.13.cloned.1.call-start
  341.6 2.5 copy.14
  344.1 116.8 %all-reduce.19.cloned.1.call-done = (f32[256,2048]{1,0:T(8,128)}, f32[512,256]{0,1:T(8,128)}) async-done(((f32[256,2048]{1,0:T(8,128)}, f32[512,256]{0,1:T(8,128)}), (f32[256,2048]{1,0:T(8,128)}, f32[512,256]{0,1:T(8,128)})) %all-reduce.19.cloned.1.call-update) | async-done | bytes 2621456 | tf_op jit(solution)/shard_map/psum | solution.py:29
  460.9 1.8 fusion.53
  462.9 11.7 %cholesky.316 = f32[128,128]{1,0:T(8,128)S(1)} custom-call(f32[128,128]{1,0:T(8,128)S(1)} %cholesky.355), custom_call_target="Cholesky" | custom-call | tf_op jit(solution)/shard_map/jit(cholesky)/cholesky | solution.py:41
  474.7 9.8 %custom-call.40 = f32[1,128,128]{1,2,0:T(8,128)S(1)} custom-call(f32[1,128,128]{2,1,0:T(8,128)S(1)} %get-tuple-element.88), custom_call_target="InvertDiagBlocksLowerTriangular" | custom-call | tf_op jit(solution)/shard_map/jit(cholesky)/cholesky | solution.py:41
  485.0 11.7 %cholesky.333 = f32[128,128]{1,0:T(8,128)S(1)} custom-call(f32[128,128]{1,0:T(8,128)S(1)} %convolution_subtract_fusion.6), custom_call_target="Cholesky" | custom-call | tf_op jit(solution)/shard_map/jit(cholesky)/cholesky | solution.py:41
  499.5 4.1 while.7
  500.1 1.4 bitcast_dynamic-update-slice_fusion.11
  502.2 1.4 bitcast_dynamic-update-slice_fusion.11
  503.6 19.7 %custom-call.33 = f32[2,128,128]{1,2,0:T(8,128)S(1)} custom-call(f32[2,128,128]{2,1,0:T(8,128)S(1)} %get-tuple-element.35), custom_call_target="InvertDiagBlocksLowerTriangular" | custom-call | tf_op jit(solution)/shard_map/jit(_cho_solve)/triangular_solve | solution.py:41
  523.3 4.8 convolution_multiply_fusion
  528.6 85.9 %all-reduce.17.cloned.1.call-done = f32[512,512]{1,0:T(8,128)} async-done(((f32[512,512]{1,0:T(8,128)}), f32[512,512]{1,0:T(8,128)}) %all-reduce.17.cloned.1.call-update) | async-done | bytes 1048592 | tf_op jit(solution)/shard_map/psum | solution.py:27
  614.5 2.3 fusion.56
  618.1 73.0 %all-reduce.13.cloned.1.call-done = f32[256,256]{0,1:T(8,128)} async-done(((f32[256,256]{0,1:T(8,128)}), f32[256,256]{0,1:T(8,128)}) %all-reduce.13.cloned.1.call-update) | async-done | bytes 262160 | tf_op jit(solution)/shard_map/psum | solution.py:31
  693.2 11.7 %cholesky.248 = f32[128,128]{1,0:T(8,128)S(1)} custom-call(f32[128,128]{1,0:T(8,128)S(1)} %cholesky.349), custom_call_target="Cholesky" | custom-call | tf_op jit(solution)/shard_map/jit(cholesky)/cholesky | solution.py:33
  705.0 9.8 %custom-call.38 = f32[1,128,128]{1,2,0:T(8,128)S(1)} custom-call(f32[1,128,128]{2,1,0:T(8,128)S(1)} %get-tuple-element.92), custom_call_target="InvertDiagBlocksLowerTriangular" | custom-call | tf_op jit(solution)/shard_map/jit(cholesky)/cholesky | solution.py:33
  716.9 11.9 %cholesky.265 = f32[128,128]{1,0:T(8,128)S(1)} custom-call(f32[128,128]{1,0:T(8,128)S(1)} %convolution_subtract_fusion.8), custom_call_target="Cholesky" | custom-call | tf_op jit(solution)/shard_map/jit(cholesky)/cholesky | solution.py:33
  731.5 4.0 while.5
  734.1 1.4 bitcast_dynamic-update-slice_fusion.9
  735.5 19.7 %custom-call.31 = f32[2,128,128]{1,2,0:T(8,128)S(1)} custom-call(f32[2,128,128]{2,1,0:T(8,128)S(1)} %get-tuple-element.19), custom_call_target="InvertDiagBlocksLowerTriangular" | custom-call | tf_op jit(solution)/shard_map/jit(_solve_triangular)/triangular_solve | solution.py:35
  755.2 2.4 fusion
  761.2 1.4 copy-done.3
  762.6 4.5 convolution_bitcast_fusion.1
  768.3 73.2 %all-reduce.15.cloned.1.call-done = f32[512,256]{0,1:T(8,128)} async-done(((f32[512,256]{0,1:T(8,128)}), f32[512,256]{0,1:T(8,128)}) %all-reduce.15.cloned.1.call-update) | async-done | bytes 524304 | tf_op jit(solution)/shard_map/psum | solution.py:37
  841.5 1.8 fusion.52
  845.9 11.9 %cholesky.282 = f32[128,128]{1,0:T(8,128)S(1)} custom-call(f32[128,128]{1,0:T(8,128)S(1)} %cholesky.352), custom_call_target="Cholesky" | custom-call | tf_op jit(solution)/shard_map/jit(cholesky)/cholesky | solution.py:43
  857.8 9.8 %custom-call.39 = f32[1,128,128]{1,2,0:T(8,128)S(1)} custom-call(f32[1,128,128]{2,1,0:T(8,128)S(1)} %get-tuple-element.84), custom_call_target="InvertDiagBlocksLowerTriangular" | custom-call | tf_op jit(solution)/shard_map/jit(cholesky)/cholesky | solution.py:43
  869.8 11.7 %cholesky.299 = f32[128,128]{1,0:T(8,128)S(1)} custom-call(f32[128,128]{1,0:T(8,128)S(1)} %convolution_subtract_fusion.7), custom_call_target="Cholesky" | custom-call | tf_op jit(solution)/shard_map/jit(cholesky)/cholesky | solution.py:43
  885.2 4.1 while.6
  885.8 1.4 bitcast_dynamic-update-slice_fusion.10
  887.9 1.4 bitcast_dynamic-update-slice_fusion.10
  890.0 20.5 %custom-call.32 = f32[2,128,128]{1,2,0:T(8,128)S(1)} custom-call(f32[2,128,128]{2,1,0:T(8,128)} %copy-done.16), custom_call_target="InvertDiagBlocksLowerTriangular" | custom-call | tf_op jit(solution)/shard_map/jit(_cho_solve)/triangular_solve | solution.py:43
  (134 shorter events, 42.4 us)
Async XLA Ops:
  7.2 302.9 %copy-start = (f32[512,1024]{1,0:T(8,128)S(1)}, f32[512,1024]{1,0:T(8,128)}, u32[]{:S(2)}) copy-start(f32[512,1024]{1,0:T(8,128)} %param.9) | copy-start | bytes 6291460
  7.2 91.5 %all-reduce.9.cloned.1.call-start = ((), (), s32[]{:S(2)}) async-start(), calls=%async_computation | async-start | bytes 2097152 | tf_op jit(solution)/shard_map/psum | solution.py:28
  17.9 84.9 %copy-start.12 = (f32[256,1024]{1,0:T(8,128)S(1)}, f32[256,1024]{1,0:T(8,128)}, u32[]{:S(2)}) copy-start(f32[256,1024]{1,0:T(8,128)} %param.8) | copy-start | bytes 3145732
  17.9 223.0 %all-reduce.11.cloned.1.call-start = ((), (), s32[]{:S(2)}) async-start(), calls=%async_computation.1 | async-start | bytes 524288 | tf_op jit(solution)/shard_map/psum | solution.py:30
  102.7 358.2 %all-reduce.19.cloned.1.call-start = ((), (), s32[]{:S(2)}) async-start(), calls=%async_computation.5 | async-start | bytes 5242880 | tf_op jit(solution)/shard_map/psum | solution.py:29
  113.5 194.2 %copy-start.4 = (f32[1024,256]{1,0:T(8,128)S(1)}, f32[1024,256]{1,0:T(8,128)}, u32[]{:S(2)}) copy-start(f32[1024,256]{1,0:T(8,128)} %all-reduce.9.cloned.1.call-done) | copy-start | bytes 3145732
  243.0 0.7 copy-start.13
  279.2 2.0 copy-start.10
  286.4 0.7 copy-start.17
  308.4 1.7 copy-start.5
  312.8 301.7 %all-reduce.17.cloned.1.call-start = ((), (), s32[]{:S(2)}) async-start(), calls=%async_computation.4 | async-start | bytes 2097152 | tf_op jit(solution)/shard_map/psum | solution.py:27
  312.9 16.9 %copy-start.2 = (f32[512,2048]{1,0:T(8,128)S(1)}, f32[512,2048]{1,0:T(8,128)}, u32[]{:S(2)}) copy-start(f32[512,2048]{1,0:T(8,128)} %param.10) | copy-start | bytes 12582916
  329.8 10.7 %copy-start.6 = (f32[128,1024]{1,0:T(8,128)S(1)}, f32[128,1024]{1,0:T(8,128)}, u32[]{:S(2)}) copy-start(f32[128,1024]{1,0:T(8,128)} %copy-done.5) | copy-start | bytes 1572868
  337.7 353.3 %all-reduce.13.cloned.1.call-start = ((), (), s32[]{:S(2)}) async-start(), calls=%async_computation.2 | async-start | bytes 524288 | tf_op jit(solution)/shard_map/psum | solution.py:31
  523.3 91.3 %copy-start.9 = (f32[512,256]{0,1:T(8,128)S(1)}, f32[512,256]{0,1:T(8,128)}, u32[]{:S(2)}) copy-start(f32[512,256]{0,1:T(8,128)} %get-tuple-element.72) | copy-start | bytes 1572868
  528.2 313.4 %all-reduce.15.cloned.1.call-start = ((), (), s32[]{:S(2)}) async-start(), calls=%async_computation.3 | async-start | bytes 1048576 | tf_op jit(solution)/shard_map/psum | solution.py:37
  693.2 11.7 %copy-start.14 = (f32[256,256]{1,0:T(8,128)}, f32[256,256]{1,0:T(8,128)S(1)}, u32[]{:S(2)}) copy-start(f32[256,256]{1,0:T(8,128)S(1)} %fusion.14) | copy-start | bytes 786436
  755.2 2.4 copy-start.1
  759.7 2.9 copy-start.3
  759.9 1.3 copy-start.7
  843.3 67.1 %copy-start.8 = (f32[512,256]{0,1:T(8,128)S(1)}, f32[512,256]{0,1:T(8,128)}, u32[]{:S(2)}) copy-start(f32[512,256]{0,1:T(8,128)} %all-reduce.15.cloned.1.call-done) | copy-start | bytes 1572868
  845.2 0.7 copy-start.15
  882.3 1.9 copy-start.11
  889.3 0.7 copy-start.16
Sparse Core Ops, SparseCore 0:
  18.1 80.5 all-reduce.8
  102.8 138.0 all-reduce.10
  313.0 147.9 all-reduce.18
  465.6 148.9 all-reduce.16
  617.4 73.6 all-reduce.12
  767.3 74.1 all-reduce.14
where the time goes:
time: 929 us; the launch traced here: 921 us
  waiting for transfers between devices  557 us (60%)
  other arithmetic  225 us (24%)
  matrix products  86.6 us (9%)
  local copies, waits for them, and re-layouts  28.3 us (3%)
  between operations  20.2 us (2%)
    psum x1, waiting for transfers between devices, per_device(): gram_y = lax.psum(inner_rows(range_full, range_full) / rows_total, 'cell')  127 us
    psum x1, waiting for transfers between devices, per_device(): co_full = lax.psum(co_term, 'cell')  117 us
    psum x1, waiting for transfers between devices, per_device(): sketch_z = lax.psum(core_term, ('cell', 'tm'))  85.9 us
    psum x1, waiting for transfers between devices, per_device(): range_full = lax.psum(range_term, 'tm')  80.7 us
    psum x1, waiting for transfers between devices, per_device(): right_image = lax.psum(inner_cols(core_right, co_basis), 'tm')  73.2 us
    psum x1, waiting for transfers between devices, per_device(): gram_w = lax.psum(inner_cols(co_full, co_full) / cols_total, 'tm')  73 us
    dot_general x5, matrix products, product(): jnp.dot(left, right, precision=lax.Precision.HIGHEST, preferred_element_t...  41.6 us
    another operation x7, other arithmetic, per_device(): jnp.linalg.cholesky(gram_right)  34.8 us
  transfers between devices with their start and end apart: 6, of which 6 were waited for; matrix products, arithmetic and copies ran while one was open for 12% of the time, Pallas kernels for 0%

commit v1 on v0

--- a/solution.py
+++ b/solution.py
@@ -25,7 +25,8 @@
     left_window = product(core_left, window)
     core_term = inner_cols(left_window, core_right)
     sketch_z = lax.psum(core_term, ("cell", "tm"))
-    range_full = lax.psum(range_term, "tm")
+    parts = lax.all_gather(range_term, "tm")
+    range_full = jnp.sum(parts, axis=0)
     co_full = lax.psum(co_term, "cell")
     gram_y = lax.psum(inner_rows(range_full, range_full) / rows_total, "cell")
     gram_w = lax.psum(inner_cols(co_full, co_full) / cols_total, "tm")

time: 929 us -> 1030 us (1.11)
  waiting for transfers between devices: 557 us -> 651 us
    all_gather x0 -> x1, waiting for transfers between devices: none -> 171 us  [per_device(): parts = lax.all_gather(range_term, 'tm')]
    psum x1 -> x0, waiting for transfers between devices: 80.7 us -> none  [per_device(): range_full = lax.psum(range_term, 'tm')]
  transfers between devices with their start and end apart: 6 -> 6, of which waited for: 6 -> 6; matrix products, arithmetic and copies ran while one was open for 12% -> 11% of each run, Pallas kernels for 0% -> 0%
where the time goes in v1:
time: 1030 us; the launch traced here: 1020 us
  waiting for transfers between devices  651 us (63%)
  other arithmetic  229 us (22%)
  matrix products  85.4 us (8%)
  local copies, waits for them, and re-layouts  28.3 us (3%)
  between operations  20.2 us (2%)
    all_gather x1, waiting for transfers between devices, per_device(): parts = lax.all_gather(range_term, 'tm')  171 us
    psum x1, waiting for transfers between devices, per_device(): gram_y = lax.psum(inner_rows(range_full, range_full) / rows_total, 'cell')  130 us
    psum x1, waiting for transfers between devices, per_device(): co_full = lax.psum(co_term, 'cell')  117 us
    psum x1, waiting for transfers between devices, per_device(): sketch_z = lax.psum(core_term, ('cell', 'tm'))  85.8 us
    psum x1, waiting for transfers between devices, per_device(): right_image = lax.psum(inner_cols(core_right, co_basis), 'tm')  73.5 us
    psum x1, waiting for transfers between devices, per_device(): gram_w = lax.psum(inner_cols(co_full, co_full) / cols_total, 'tm')  73 us
    dot_general x5, matrix products, product(): jnp.dot(left, right, precision=lax.Precision.HIGHEST, preferred_element_t...  41.9 us
    another operation x7, other arithmetic, per_device(): jnp.linalg.cholesky(gram_right)  34.8 us
  transfers between devices with their start and end apart: 6, of which 6 were waited for; matrix products, arithmetic and copies ran while one was open for 11% of the time, Pallas kernels for 0%

profile of v1, /device:TPU:0, one launch (start us, length us, event | category | flops | bytes accessed | tf_op | source)
XLA Modules:
  0.0 1017.1 jit_solution(13753096916916904676)
XLA Ops:
  7.2 10.7 %fusion.50 = f32[1024,256]{1,0:T(8,128)} fusion(f32[1024,2048]{1,0:T(8,128)} %param.6, f32[2048,256]{1,0:T(8,128)} %param.7), kind=kOutput, calls=%fused_computation.123 | convolution fusion | flops 6442450944 | bytes 11534336 | tf_op jit(solution)/shard_map/dot_general | solution.py:17
  18.0 171.0 %all-gather.3.cloned.1.call-done = f32[8192,256]{1,0:T(8,128)} async-done(((f32[1024,256]{1,0:T(8,128)}), f32[8192,256]{1,0:T(8,128)}) %all-gather.3.cloned.1.call-update) | async-done | bytes 8388624 | tf_op jit(solution)/shard_map/all_gather | solution.py:28
  188.9 4.1 reduce_sum.9
  193.0 2.5 convolution_multiply_fusion.1
  195.6 11.0 %fusion.51 = f32[256,2048]{1,0:T(8,128)} fusion(f32[256,1024]{1,0:T(8,128)} %param.8, f32[1024,2048]{1,0:T(8,128)} %param.6), kind=kOutput, calls=%fused_computation.124 | convolution fusion | flops 6442450944 | bytes 11534336 | tf_op jit(solution)/shard_map/dot_general | solution.py:17
  206.6 130.5 %all-reduce.8.cloned.1.call-done = f32[256,256]{0,1:T(8,128)} async-done(((f32[256,256]{0,1:T(8,128)}), f32[256,256]{0,1:T(8,128)}) %all-reduce.8.cloned.1.call-update) | async-done | bytes 262160 | tf_op jit(solution)/shard_map/psum | solution.py:31
  339.9 11.7 %cholesky.214 = f32[128,128]{1,0:T(8,128)S(1)} custom-call(f32[128,128]{1,0:T(8,128)S(1)} %cholesky.346), custom_call_target="Cholesky" | custom-call | tf_op jit(solution)/shard_map/jit(cholesky)/cholesky | solution.py:33
  351.6 9.8 custom-call.37
  363.6 11.7 %cholesky.231 = f32[128,128]{1,0:T(8,128)S(1)} custom-call(f32[128,128]{1,0:T(8,128)S(1)} %convolution_subtract_fusion.9), custom_call_target="Cholesky" | custom-call | tf_op jit(solution)/shard_map/jit(cholesky)/cholesky | solution.py:33
  378.4 4.1 while.4
  379.1 1.4 bitcast_dynamic-update-slice_fusion.8
  381.1 1.4 bitcast_dynamic-update-slice_fusion.8
  383.2 20.7 %custom-call.30 = f32[2,128,128]{1,2,0:T(8,128)S(1)} custom-call(f32[2,128,128]{2,1,0:T(8,128)} %copy-done.15), custom_call_target="InvertDiagBlocksLowerTriangular" | custom-call | tf_op jit(solution)/shard_map/jit(_solve_triangular)/triangular_solve | solution.py:35
  406.2 2.8 convolution_bitcast_fusion
  409.1 16.9 %fusion.54 = f32[512,2048]{1,0:T(8,128)S(1)} fusion(f32[512,1024]{1,0:T(8,128)S(1)} %copy-done, f32[1024,2048]{1,0:T(8,128)} %param.6), kind=kOutput, calls=%fused_computation.127 | convolution fusion | flops 12884901888 | bytes 14680064 | tf_op jit(solution)/shard_map/dot_general | solution.py:17
  426.0 7.9 fusion.55
  433.9 2.8 all-reduce.10.cloned.1.call-start
  437.7 2.5 copy.14
  440.3 116.8 %all-reduce.16.cloned.1.call-done = (f32[256,2048]{1,0:T(8,128)}, f32[512,256]{0,1:T(8,128)}) async-done(((f32[256,2048]{1,0:T(8,128)}, f32[512,256]{0,1:T(8,128)}), (f32[256,2048]{1,0:T(8,128)}, f32[512,256]{0,1:T(8,128)})) %all-reduce.16.cloned.1.call-update) | async-done | bytes 2621456 | tf_op jit(solution)/shard_map/psum | solution.py:30
  557.1 1.8 fusion.53
  559.1 11.7 %cholesky.316 = f32[128,128]{1,0:T(8,128)S(1)} custom-call(f32[128,128]{1,0:T(8,128)S(1)} %cholesky.355), custom_call_target="Cholesky" | custom-call | tf_op jit(solution)/shard_map/jit(cholesky)/cholesky | solution.py:42
  570.9 9.8 custom-call.40
  581.2 11.7 %cholesky.333 = f32[128,128]{1,0:T(8,128)S(1)} custom-call(f32[128,128]{1,0:T(8,128)S(1)} %convolution_subtract_fusion.6), custom_call_target="Cholesky" | custom-call | tf_op jit(solution)/shard_map/jit(cholesky)/cholesky | solution.py:42
  595.7 4.1 while.7
  596.3 1.4 bitcast_dynamic-update-slice_fusion.11
  598.3 1.4 bitcast_dynamic-update-slice_fusion.11
  599.8 19.7 %custom-call.33 = f32[2,128,128]{1,2,0:T(8,128)S(1)} custom-call(f32[2,128,128]{2,1,0:T(8,128)S(1)} %get-tuple-element.35), custom_call_target="InvertDiagBlocksLowerTriangular" | custom-call | tf_op jit(solution)/shard_map/jit(_cho_solve)/triangular_solve | solution.py:42
  619.5 4.8 convolution_multiply_fusion
  624.8 85.8 %all-reduce.14.cloned.1.call-done = f32[512,512]{1,0:T(8,128)} async-done(((f32[512,512]{1,0:T(8,128)}), f32[512,512]{1,0:T(8,128)}) %all-reduce.14.cloned.1.call-update) | async-done | bytes 1048592 | tf_op jit(solution)/shard_map/psum | solution.py:27
  710.5 2.3 fusion.56
  714.0 73.0 %all-reduce.10.cloned.1.call-done = f32[256,256]{0,1:T(8,128)} async-done(((f32[256,256]{0,1:T(8,128)}), f32[256,256]{0,1:T(8,128)}) %all-reduce.10.cloned.1.call-update) | async-done | bytes 262160 | tf_op jit(solution)/shard_map/psum | solution.py:32
  789.2 11.7 %cholesky.248 = f32[128,128]{1,0:T(8,128)S(1)} custom-call(f32[128,128]{1,0:T(8,128)S(1)} %cholesky.349), custom_call_target="Cholesky" | custom-call | tf_op jit(solution)/shard_map/jit(cholesky)/cholesky | solution.py:34
  801.0 9.8 custom-call.38
  812.9 11.9 %cholesky.265 = f32[128,128]{1,0:T(8,128)S(1)} custom-call(f32[128,128]{1,0:T(8,128)S(1)} %convolution_subtract_fusion.8), custom_call_target="Cholesky" | custom-call | tf_op jit(solution)/shard_map/jit(cholesky)/cholesky | solution.py:34
  827.5 4.0 while.5
  831.5 19.7 %custom-call.31 = f32[2,128,128]{1,2,0:T(8,128)S(1)} custom-call(f32[2,128,128]{2,1,0:T(8,128)S(1)} %get-tuple-element.19), custom_call_target="InvertDiagBlocksLowerTriangular" | custom-call | tf_op jit(solution)/shard_map/jit(_solve_triangular)/triangular_solve | solution.py:36
  851.2 2.4 fusion
  857.2 1.4 copy-done.3
  858.6 4.5 convolution_bitcast_fusion.1
  864.3 73.5 %all-reduce.12.cloned.1.call-done = f32[512,256]{0,1:T(8,128)} async-done(((f32[512,256]{0,1:T(8,128)}), f32[512,256]{0,1:T(8,128)}) %all-reduce.12.cloned.1.call-update) | async-done | bytes 524304 | tf_op jit(solution)/shard_map/psum | solution.py:38
  937.8 1.8 fusion.52
  942.2 11.9 %cholesky.282 = f32[128,128]{1,0:T(8,128)S(1)} custom-call(f32[128,128]{1,0:T(8,128)S(1)} %cholesky.352), custom_call_target="Cholesky" | custom-call | tf_op jit(solution)/shard_map/jit(cholesky)/cholesky | solution.py:44
  954.1 9.8 custom-call.39
  966.1 11.7 %cholesky.299 = f32[128,128]{1,0:T(8,128)S(1)} custom-call(f32[128,128]{1,0:T(8,128)S(1)} %convolution_subtract_fusion.7), custom_call_target="Cholesky" | custom-call | tf_op jit(solution)/shard_map/jit(cholesky)/cholesky | solution.py:44
  981.5 4.1 while.6
  982.1 1.4 bitcast_dynamic-update-slice_fusion.10
  984.1 1.4 bitcast_dynamic-update-slice_fusion.10
  986.2 20.5 %custom-call.32 = f32[2,128,128]{1,2,0:T(8,128)S(1)} custom-call(f32[2,128,128]{2,1,0:T(8,128)} %copy-done.14), custom_call_target="InvertDiagBlocksLowerTriangular" | custom-call | tf_op jit(solution)/shard_map/jit(_cho_solve)/triangular_solve | solution.py:44
  (131 shorter events, 43.8 us)
Async XLA Ops:
  7.2 399.0 %copy-start = (f32[512,1024]{1,0:T(8,128)S(1)}, f32[512,1024]{1,0:T(8,128)}, u32[]{:S(2)}) copy-start(f32[512,1024]{1,0:T(8,128)} %param.9) | copy-start | bytes 6291460
  7.2 181.8 %all-gather.3.cloned.1.call-start = ((), (), s32[]{:S(2)}) async-start(), calls=%async_computation.4 | async-start | bytes 9437184 | tf_op jit(solution)/shard_map/all_gather | solution.py:28
  17.9 319.2 %all-reduce.8.cloned.1.call-start = ((), (), s32[]{:S(2)}) async-start(), calls=%async_computation | async-start | bytes 524288 | tf_op jit(solution)/shard_map/psum | solution.py:31
  195.6 361.5 %all-reduce.16.cloned.1.call-start = ((), (), s32[]{:S(2)}) async-start(), calls=%async_computation.5 | async-start | bytes 5242880 | tf_op jit(solution)/shard_map/psum | solution.py:30
  339.2 0.7 copy-start.11
  375.4 2.0 copy-start.9
  382.5 0.7 copy-start.15
  404.5 1.7 copy-start.4
  409.0 301.5 %all-reduce.14.cloned.1.call-start = ((), (), s32[]{:S(2)}) async-start(), calls=%async_computation.3 | async-start | bytes 2097152 | tf_op jit(solution)/shard_map/psum | solution.py:27
  409.0 16.9 %copy-start.2 = (f32[512,2048]{1,0:T(8,128)S(1)}, f32[512,2048]{1,0:T(8,128)}, u32[]{:S(2)}) copy-start(f32[512,2048]{1,0:T(8,128)} %param.10) | copy-start | bytes 12582916
  426.0 10.7 %copy-start.5 = (f32[128,1024]{1,0:T(8,128)S(1)}, f32[128,1024]{1,0:T(8,128)}, u32[]{:S(2)}) copy-start(f32[128,1024]{1,0:T(8,128)} %copy-done.4) | copy-start | bytes 1572868
  433.9 353.2 %all-reduce.10.cloned.1.call-start = ((), (), s32[]{:S(2)}) async-start(), calls=%async_computation.1 | async-start | bytes 524288 | tf_op jit(solution)/shard_map/psum | solution.py:32
  619.4 91.1 %copy-start.8 = (f32[512,256]{0,1:T(8,128)S(1)}, f32[512,256]{0,1:T(8,128)}, u32[]{:S(2)}) copy-start(f32[512,256]{0,1:T(8,128)} %get-tuple-element.72) | copy-start | bytes 1572868
  624.3 313.5 %all-reduce.12.cloned.1.call-start = ((), (), s32[]{:S(2)}) async-start(), calls=%async_computation.2 | async-start | bytes 1048576 | tf_op jit(solution)/shard_map/psum | solution.py:38
  789.1 11.7 %copy-start.12 = (f32[256,256]{1,0:T(8,128)}, f32[256,256]{1,0:T(8,128)S(1)}, u32[]{:S(2)}) copy-start(f32[256,256]{1,0:T(8,128)S(1)} %fusion.14) | copy-start | bytes 786436
  851.2 2.4 copy-start.1
  855.7 2.9 copy-start.3
  855.9 1.3 copy-start.6
  939.6 67.1 %copy-start.7 = (f32[512,256]{0,1:T(8,128)S(1)}, f32[512,256]{0,1:T(8,128)}, u32[]{:S(2)}) copy-start(f32[512,256]{0,1:T(8,128)} %all-reduce.12.cloned.1.call-done) | copy-start | bytes 1572868
  941.4 0.7 copy-start.13
  978.6 1.9 copy-start.10
  985.6 0.7 copy-start.14
Sparse Core Ops, SparseCore 0:
  18.1 170.8 all-gather.2
  195.7 141.3 all-reduce.7
  409.1 147.9 all-reduce.15
  561.7 148.7 all-reduce.13
  713.4 73.6 all-reduce.9
  863.3 74.4 all-reduce.11
